TPU v7x, 32 devices: a whole 2x2x4 slice. The times are simulated.
32 devices in a mesh: row: 8 (over z, y), col: 4 (over x, core).
Axes of the slice: x: 2, y: 2, z: 4, core: 2. Of those that a mesh axis runs over, the one named last changes fastest.
Arguments:
- basis_values: bfloat16 [4, 4096, 4096], P(None, 'row', 'col'), may hold values from -6 to 6
- density: float32 [4096, 2560], P('row'), may hold values from -1 to 1, as said below
- screen: int32 [32, 32], P('row', 'col'), may hold values 0 or 1
- atom_of_block: int32 [32], P('col'), may hold values from 0 to 63
- atom_factor: float32 [64], replicated, may hold values from 0.5 to 2
- quad_weight: float32 [4096], P('col'), may hold values from 0.5 to 2
- core_density: float32 [4096], P('col'), may hold values from 0.3 to 1
Outputs:
- xc_matrix: float32 [4096, 1536], P(('row', 'col'))
Inputs may be any that keep to these rules, and one draw needn't show every extreme that they name: The density matrix is symmetric. Column block k of a row (k from 0 to 4, 512 columns each) holds the row's entries with the basis block k - 2 places further along the closed chain of 8 blocks; all other entries are zero.
All inputs are finite; a program needn't handle non-finite values. No bound on the sum of `screen` on one device may be relied on, other than what follows from the above.
Results may differ from a plain program's by a relative error of at most 0.0014.
Values may be sent and summed in bfloat16 or wider, within the bound.
No kernel may reach another device: no remote copies, remote signals or barrier semaphores. Data moves between devices by JAX's collectives and lax.ppermute only.
A program may use at most 64 MiB of HBM per device.

v0:
```python
import math
import jax
import jax.numpy as jnp
from jax import lax
from jax.sharding import PartitionSpec as P

BAND = 5
KAPPA_VALUE = 0.804
MU_VALUE = 0.22
SLATER_COEF = 0.7386


def from_behind(block, axis, distance):
    devices = range(lax.axis_size(axis))
    route = [((i - distance) % len(devices), i) for i in devices]
    return lax.ppermute(block, axis, route)


def energy_density(density_in, squared_in, core):
    regular = jnp.sqrt(density_in * density_in + core * core)
    reduced = squared_in * regular ** (-8.0 / 3.0)
    enhance = 1.0 + KAPPA_VALUE - KAPPA_VALUE / (1.0 + MU_VALUE * reduced / KAPPA_VALUE)
    return -SLATER_COEF * regular ** (4.0 / 3.0) * enhance


def potentials(density_in, squared_in, core):

    def total_energy(first_arg, second_arg):
        return jnp.sum(energy_density(first_arg, second_arg, core))

    return jax.grad(total_energy, argnums=(0, 1))(density_in, squared_in)


def masked_basis(basis_values, screen):
    components, row_count, points = basis_values.shape
    row_blocks, point_blocks = screen.shape
    shaped = basis_values.reshape(
        components, row_blocks, row_count // row_blocks, point_blocks, points // point_blocks
    )
    keeper = screen.astype(basis_values.dtype)[None, :, None, :, None]
    return (shaped * keeper).reshape(components, row_count, points)


def contract(left_side, right_side):
    return lax.dot_general(
        left_side, right_side, (((1,), (1,)), ((), ())), preferred_element_type=jnp.float32
    )


def body(basis_values, density, screen, atom_of_block, atom_factor, quad_weight, core_density):
    masked = masked_basis(basis_values, screen)
    values = masked[0]
    row_count, points = values.shape
    reach = BAND // 2
    nearby = {0: values}
    for heading in (1, -1):
        current = values
        for stride in range(1, reach + 1):
            current = from_behind(current, "row", -heading)
            nearby[heading * stride] = current
    applied = jnp.zeros((row_count, points), jnp.float32)
    for offset in range(-reach, reach + 1):
        column = offset + reach
        strip = density[:, column * row_count : (column + 1) * row_count]
        applied = applied + jnp.dot(
            strip, nearby[offset].astype(jnp.float32), precision=lax.Precision.HIGHEST
        )
    masked32 = masked.astype(jnp.float32)
    partial_sums = jnp.einsum("cmg,mg->cg", masked32, applied, precision=lax.Precision.HIGHEST)
    summed = lax.psum(partial_sums, "row")
    point_density = summed[0]
    gradient = 2.0 * summed[1:]
    squared = jnp.sum(gradient * gradient, axis=0)
    atoms = atom_factor.shape[0]
    chooser = (atom_of_block[:, None] == jnp.arange(atoms, dtype=jnp.int32)[None, :]).astype(
        jnp.float32
    )
    block_factor = jnp.dot(chooser, atom_factor, precision=lax.Precision.HIGHEST)
    group_size = points // atom_of_block.shape[0]
    weights = (quad_weight.reshape(-1, group_size) * block_factor[:, None]).reshape(
        points
    ) / math.sqrt(points * lax.axis_size("col"))
    density_pot, gradient_pot = potentials(point_density, squared, core_density)
    scalar_part = 0.5 * weights * density_pot
    vector_part = 2.0 * weights * gradient_pot * gradient
    half_pot = (
        scalar_part * masked32[0] + jnp.sum(vector_part[:, None, :] * masked32[1:], axis=0)
    ).astype(jnp.bfloat16)
    pieces = [contract(half_pot, values) + contract(values, half_pot)]
    for local_offset in range(1, reach + 1):
        pieces.append(contract(half_pot, nearby[local_offset]))
    for local_offset in range(1, reach + 1):
        lower_rows = nearby[-local_offset]
        pieces.append(contract(lower_rows, half_pot))
    summed_terms = lax.psum_scatter(
        jnp.concatenate(pieces, axis=1), "col", scatter_dimension=0, tiled=True
    )
    result = [summed_terms[:, :row_count]]
    for offset in range(1, reach + 1):
        start_col = (reach + offset) * row_count
        mirrored = from_behind(
            summed_terms[:, start_col : start_col + row_count].astype(jnp.bfloat16), "row", -offset
        ).astype(jnp.float32)
        result.append(summed_terms[:, offset * row_count : (offset + 1) * row_count] + mirrored)
    return jnp.concatenate(result, axis=1)


def solution(mesh):
    in_specs = (
        P(None, "row", "col"),
        P("row", None),
        P("row", "col"),
        P("col"),
        P(),
        P("col"),
        P("col"),
    )
    out_specs = P(("row", "col"), None)
    return jax.shard_map(body, mesh=mesh, in_specs=in_specs, out_specs=out_specs, check_vma=False)
```

profile of v0, /device:TPU:0, one launch (start us, length us, event | category | flops | bytes accessed | tf_op | source)
XLA Modules:
  0.0 244.4 jit_solution(6484854692076097885)
XLA Ops:
  6.5 0.0 copy-start
  6.5 0.0 reduce-scatter.2.cloned.1.call-start
  6.5 0.7 convert_element_type.29
  7.2 3.3 %copy.18 = bf16[256,8,8,128]{3,2,1,0:T(8,128)(2,1)S(1)} copy(bf16[256,8,8,128]{3,1,2,0:T(8,128)(2,1)} %bitcast.64) | data formatting | bytes 8388608
  10.5 0.0 copy-start.1
  10.5 0.1 slice_multiply_fusion.1
  10.7 0.3 copy.27
  10.9 3.0 %collective-permute-start = (bf16[512,1024]{1,0:T(8,128)(2,1)S(1)}, bf16[512,1024]{1,0:T(8,128)(2,1)S(1)}, u32[]{:S(2)}, u32[]{:S(2)}) collective-permute-start(bf16[512,1024]{1,0:T(8,128)(2,1)S(1)} %bitcast.75), channel_id=1, source_target_pairs={{28,0},{0,4},{4,8},{8,12},{12,16},{16,20},{20,24},{24,28},{29,1},{... | collective-permute-start | bytes 3145736 | tf_op jit(solution)/shard_map/ppermute | solution.py:16
  14.0 3.1 %collective-permute-start.2 = (bf16[512,1024]{1,0:T(8,128)(2,1)S(1)}, bf16[512,1024]{1,0:T(8,128)(2,1)S(1)}, u32[]{:S(2)}, u32[]{:S(2)}) collective-permute-start(bf16[512,1024]{1,0:T(8,128)(2,1)S(1)} %bitcast.76), channel_id=1, source_target_pairs={{4,0},{8,4},{12,8},{16,12},{20,16},{24,20},{28,24},{0,28},{5,1},{9... | collective-permute-start | bytes 3145736 | tf_op jit(solution)/shard_map/ppermute | solution.py:16
  17.1 0.2 mul.148
  17.3 0.0 slice-start
  17.3 0.3 copy.26
  17.6 0.0 copy-done.1
  17.6 0.0 slice-start.1
  17.6 4.2 %multiply_convert_fusion = f32[4,512,1024]{2,1,0:T(8,128)} fusion(bf16[4,512,1024]{2,1,0:T(8,128)(2,1)S(1)} %copy-done.1, bf16[512,1024]{1,0:T(8,128)(2,1)S(1)} %bitcast.69), kind=kLoop, calls=%fused_computation.3 | loop fusion | flops 4194304 | bytes 13631488 | tf_op jit(solution)/shard_map/convert_element_type | solution.py:68
  21.8 37.1 %collective-permute-done = bf16[512,1024]{1,0:T(8,128)(2,1)S(1)} collective-permute-done((bf16[512,1024]{1,0:T(8,128)(2,1)S(1)}, bf16[512,1024]{1,0:T(8,128)(2,1)S(1)}, u32[]{:S(2)}, u32[]{:S(2)}) %collective-permute-start) | collective-permute-done | bytes 1048608 | tf_op jit(solution)/shard_map/ppermute | solution.py:16
  58.9 2.5 %collective-permute-start.1 = (bf16[512,1024]{1,0:T(8,128)(2,1)S(1)}, bf16[512,1024]{1,0:T(8,128)(2,1)S(1)}, u32[]{:S(2)}, u32[]{:S(2)}) collective-permute-start(bf16[512,1024]{1,0:T(8,128)(2,1)S(1)} %collective-permute-done), channel_id=1, source_target_pairs={{28,0},{0,4},{4,8},{8,12},{12,16},{16,20},{20,24},{24,28},{29,1},{... | collective-permute-start | bytes 3145736 | tf_op jit(solution)/shard_map/ppermute | solution.py:16
  61.4 0.0 slice-done
  61.4 0.0 slice-done.1
  61.4 2.2 fusion.9
  63.6 0.0 collective-permute-done.2
  63.6 0.0 copy-start.4
  63.6 3.3 %collective-permute-start.3 = (bf16[512,1024]{1,0:T(8,128)(2,1)S(1)}, bf16[512,1024]{1,0:T(8,128)(2,1)S(1)}, u32[]{:S(2)}, u32[]{:S(2)}) collective-permute-start(bf16[512,1024]{1,0:T(8,128)(2,1)S(1)} %collective-permute-done.2), channel_id=1, source_target_pairs={{4,0},{8,4},{12,8},{16,12},{20,16},{24,20},{28,24},{0,28},{5,1},{9... | collective-permute-start | bytes 3145736 | tf_op jit(solution)/shard_map/ppermute | solution.py:16
  66.9 0.0 copy-done
  66.9 0.0 copy-done.10
  66.9 0.2 convolution_bitcast_fusion
  67.1 2.2 fusion.11
  69.3 0.0 copy-done.2
  69.3 2.2 fusion.7
  71.5 0.0 copy-done.4
  71.5 33.9 %collective-permute-done.1 = bf16[512,1024]{1,0:T(8,128)(2,1)S(1)} collective-permute-done((bf16[512,1024]{1,0:T(8,128)(2,1)S(1)}, bf16[512,1024]{1,0:T(8,128)(2,1)S(1)}, u32[]{:S(2)}, u32[]{:S(2)}) %collective-permute-start.1) | collective-permute-done | bytes 1048608 | tf_op jit(solution)/shard_map/ppermute | solution.py:16
  105.4 1.1 copy-done.6
  106.5 2.2 fusion.13
  108.7 0.5 collective-permute-done.3
  109.2 3.9 %add_add_fusion = f32[1024,512]{1,0:T(8,128)} fusion(f32[1024,512]{1,0:T(8,128)S(1)} %fusion.7, f32[1024,512]{1,0:T(8,128)S(1)} %fusion.9, f32[1024,512]{1,0:T(8,128)S(1)} %fusion.13, f32[1024,512]{1,0:T(8,128)S(1)} %fusion.11, bf16[512,1024]{1,0:T(8,128)(2,1)S(1)} %collective-permute-done.3, f32[512,2560]{1,0:T(8,128)S(1)} %bitcast.73), kind=kOutput, calls=%fused_computation.9 | convolution fusion | flops 3223322624 | bytes 12582912 | tf_op jit(solution)/shard_map/dot_general | solution.py:65
  113.1 2.9 %copy.16 = f32[1024,512]{0,1:T(8,128)} copy(f32[1024,512]{1,0:T(8,128)} %add_add_fusion) | data formatting | bytes 4194304
  116.0 4.3 %multiply_reduce_fusion = f32[1024,4]{0,1:T(4,128)S(1)} fusion(f32[1024,512]{0,1:T(8,128)} %copy.16, bf16[4,512,1024]{2,1,0:T(8,128)(2,1)} %param.7, bf16[512,1024]{1,0:T(8,128)(2,1)S(1)} %bitcast.70), kind=kLoop, calls=%fused_computation | loop fusion | flops 8384512 | bytes 7356416 | tf_op jit(solution)/shard_map/cmg,mg->cg/dot_general | solution.py:69
  120.3 37.9 %psum.7 = f32[4,1024]{1,0:T(4,128)S(1)} all-reduce(f32[4,1024]{1,0:T(4,128)S(1)} %bitcast.77), channel_id=1, replica_groups=mesh['row'=8,'col'=4] {'row'}, use_global_device_ids=true, to_apply=%region_0.0 | all-reduce | flops 4096 | bytes 32768 | tf_op jit(solution)/shard_map/psum | solution.py:70
  158.2 0.0 copy-done.8
  158.2 0.0 copy-done.9
  158.2 0.1 multiply_multiply_fusion
  158.3 3.9 %fusion = f32[512,1024]{1,0:T(8,128)S(1)} fusion(f32[4,512,1024]{2,1,0:T(8,128)} %multiply_convert_fusion, f32[3,1024]{1,0:T(4,128)S(1)} %slice_multiply_fusion.2), kind=kLoop, calls=%fused_computation.2 | loop fusion | flops 2621440 | bytes 8400896 | tf_op jit(solution)/shard_map/reduce_sum | solution.py:87
  162.3 1.9 fusion.2
  164.2 1.9 fusion.5
  166.1 0.0 copy-start.5
  166.1 0.8 fusion.17
  166.8 1.7 fusion.4
  168.6 0.0 copy-done.5
  168.6 1.7 convolution_dynamic-update-slice_fusion.3
  170.3 1.7 convolution_dynamic-update-slice_fusion.2
  172.0 0.0 copy-done.3
  172.0 1.8 convolution_dynamic-update-slice_fusion.1
  173.8 0.0 copy-done.7
  173.8 1.7 convolution_dynamic-update-slice_fusion
  175.5 0.0 reduce-scatter.2.cloned.1.call-update
  175.5 48.5 %reduce-scatter.2.cloned.1.call-done = f32[128,2560]{0,1:T(8,128)} async-done(((f32[512,2560]{0,1:T(8,128)}), f32[128,2560]{0,1:T(8,128)}) %reduce-scatter.2.cloned.1.call-update) | async-done | bytes 1310736 | tf_op jit(solution)/shard_map/reduce_scatter | solution.py:95
  224.1 1.4 convert.4
  225.5 4.3 %collective-permute-start.4 = (bf16[128,512]{0,1:T(8,128)(2,1)S(1)}, bf16[128,512]{0,1:T(8,128)(2,1)S(1)}, u32[]{:S(2)}, u32[]{:S(2)}) collective-permute-start(bf16[128,512]{0,1:T(8,128)(2,1)S(1)} %get-tuple-element.8), channel_id=1, source_target_pairs={{4,0},{8,4},{12,8},{16,12},{20,16},{24,20},{28,24},{0,28},{5,1},{9... | collective-permute-start | bytes 393224 | tf_op jit(solution)/shard_map/ppermute | solution.py:16
  229.8 0.5 collective-permute-start.5
  230.3 3.4 %collective-permute-done.4 = bf16[128,512]{0,1:T(8,128)(2,1)S(1)} collective-permute-done((bf16[128,512]{0,1:T(8,128)(2,1)S(1)}, bf16[128,512]{0,1:T(8,128)(2,1)S(1)}, u32[]{:S(2)}, u32[]{:S(2)}) %collective-permute-start.4) | collective-permute-done | bytes 131104 | tf_op jit(solution)/shard_map/ppermute | solution.py:16
  233.7 1.5 collective-permute-done.5
  235.2 1.2 fusion.18
  236.4 0.1 pad_maximum_fusion
  236.4 1.1 copy.8
  (12 shorter events, 0.1 us)
Async XLA Ops:
  6.5 60.4 %copy-start = (f32[64]{0:T(128)S(1)}, f32[64]{0:T(128)}, u32[]{:S(2)}) copy-start(f32[64]{0:T(128)} %param.11) | copy-start | bytes 772
  6.5 217.5 %reduce-scatter.2.cloned.1.call-start = ((), (), s32[]{:S(2)}) async-start(), calls=%async_computation.1 | async-start | bytes 6553600 | tf_op jit(solution)/shard_map/reduce_scatter | solution.py:95
  10.5 7.1 %copy-start.1 = (bf16[4,512,1024]{2,1,0:T(8,128)(2,1)S(1)}, bf16[4,512,1024]{2,1,0:T(8,128)(2,1)}, u32[]{:S(2)}) copy-start(bf16[4,512,1024]{2,1,0:T(8,128)(2,1)} %param.7) | copy-start | bytes 12582916
  10.9 47.9 %collective-permute-start = (bf16[512,1024]{1,0:T(8,128)(2,1)S(1)}, bf16[512,1024]{1,0:T(8,128)(2,1)S(1)}, u32[]{:S(2)}, u32[]{:S(2)}) collective-permute-start(bf16[512,1024]{1,0:T(8,128)(2,1)S(1)} %bitcast.75), channel_id=1, source_target_pairs={{28,0},{0,4},{4,8},{8,12},{12,16},{16,20},{20,24},{24,28},{29,1},{... | collective-permute-start | bytes 3145736 | tf_op jit(solution)/shard_map/ppermute | solution.py:16
  14.0 49.6 %collective-permute-start.2 = (bf16[512,1024]{1,0:T(8,128)(2,1)S(1)}, bf16[512,1024]{1,0:T(8,128)(2,1)S(1)}, u32[]{:S(2)}, u32[]{:S(2)}) collective-permute-start(bf16[512,1024]{1,0:T(8,128)(2,1)S(1)} %bitcast.76), channel_id=1, source_target_pairs={{4,0},{8,4},{12,8},{16,12},{20,16},{24,20},{28,24},{0,28},{5,1},{9... | collective-permute-start | bytes 3145736 | tf_op jit(solution)/shard_map/ppermute | solution.py:16
  17.3 44.1 %slice-start = ((s8[5242880]{0:T(1024)(128)(4,1)}), s8[4194304]{0:T(1024)(128)(4,1)S(1)}, s32[]{:S(2)}) async-start(s8[5242880]{0:T(1024)(128)(4,1)} %bitcast.72), calls=%async_computation.2 | async-start | bytes 8388608
  17.6 43.8 %slice-start.1 = ((s8[5242880]{0:T(1024)(128)(4,1)}), s8[1048576]{0:T(1024)(128)(4,1)S(1)}, s32[]{:S(2)}) async-start(s8[5242880]{0:T(1024)(128)(4,1)} %bitcast.72), calls=%async_computation.3 | async-start | bytes 2097152
  21.8 45.1 %copy-start.10 = (s32[8]{0:T(128)S(1)}, s32[8]{0:T(128)}, u32[]{:S(2)}) copy-start(s32[8]{0:T(128)} %param.10) | copy-start | bytes 100
  58.9 10.4 %copy-start.2 = (bf16[512,1024]{1,0:T(8,128)(2,1)}, bf16[512,1024]{1,0:T(8,128)(2,1)S(1)}, u32[]{:S(2)}) copy-start(bf16[512,1024]{1,0:T(8,128)(2,1)S(1)} %collective-permute-done) | copy-start | bytes 3145732
  58.9 46.5 %collective-permute-start.1 = (bf16[512,1024]{1,0:T(8,128)(2,1)S(1)}, bf16[512,1024]{1,0:T(8,128)(2,1)S(1)}, u32[]{:S(2)}, u32[]{:S(2)}) collective-permute-start(bf16[512,1024]{1,0:T(8,128)(2,1)S(1)} %collective-permute-done), channel_id=1, source_target_pairs={{28,0},{0,4},{4,8},{8,12},{12,16},{16,20},{20,24},{24,28},{29,1},{... | collective-permute-start | bytes 3145736 | tf_op jit(solution)/shard_map/ppermute | solution.py:16
  63.6 7.9 %copy-start.4 = (bf16[512,1024]{1,0:T(8,128)(2,1)}, bf16[512,1024]{1,0:T(8,128)(2,1)S(1)}, u32[]{:S(2)}) copy-start(bf16[512,1024]{1,0:T(8,128)(2,1)S(1)} %collective-permute-done.2) | copy-start | bytes 3145732
  63.6 45.6 %collective-permute-start.3 = (bf16[512,1024]{1,0:T(8,128)(2,1)S(1)}, bf16[512,1024]{1,0:T(8,128)(2,1)S(1)}, u32[]{:S(2)}, u32[]{:S(2)}) collective-permute-start(bf16[512,1024]{1,0:T(8,128)(2,1)S(1)} %collective-permute-done.2), channel_id=1, source_target_pairs={{4,0},{8,4},{12,8},{16,12},{20,16},{24,20},{28,24},{0,28},{5,1},{9... | collective-permute-start | bytes 3145736 | tf_op jit(solution)/shard_map/ppermute | solution.py:16
  105.4 1.1 copy-start.6
  116.0 42.2 %copy-start.8 = (f32[1024]{0:T(1024)S(1)}, f32[1024]{0:T(1024)}, u32[]{:S(2)}) copy-start(f32[1024]{0:T(1024)} %param.12) | copy-start | bytes 12292
  116.0 42.2 %copy-start.9 = (f32[1024]{0:T(1024)S(1)}, f32[1024]{0:T(1024)}, u32[]{:S(2)}) copy-start(f32[1024]{0:T(1024)} %param.13) | copy-start | bytes 12292
  166.1 2.5 %copy-start.5 = (bf16[512,1024]{1,0:T(8,128)(2,1)S(1)}, bf16[512,1024]{1,0:T(8,128)(2,1)}, u32[]{:S(2)}) copy-start(bf16[512,1024]{1,0:T(8,128)(2,1)} %copy-done.4) | copy-start | bytes 3145732
  168.6 3.5 %copy-start.3 = (bf16[512,1024]{1,0:T(8,128)(2,1)S(1)}, bf16[512,1024]{1,0:T(8,128)(2,1)}, u32[]{:S(2)}) copy-start(bf16[512,1024]{1,0:T(8,128)(2,1)} %copy-done.2) | copy-start | bytes 3145732
  170.3 3.5 %copy-start.7 = (bf16[512,1024]{1,0:T(8,128)(2,1)S(1)}, bf16[512,1024]{1,0:T(8,128)(2,1)}, u32[]{:S(2)}) copy-start(bf16[512,1024]{1,0:T(8,128)(2,1)} %copy-done.6) | copy-start | bytes 3145732
  225.5 8.2 %collective-permute-start.4 = (bf16[128,512]{0,1:T(8,128)(2,1)S(1)}, bf16[128,512]{0,1:T(8,128)(2,1)S(1)}, u32[]{:S(2)}, u32[]{:S(2)}) collective-permute-start(bf16[128,512]{0,1:T(8,128)(2,1)S(1)} %get-tuple-element.8), channel_id=1, source_target_pairs={{4,0},{8,4},{12,8},{16,12},{20,16},{24,20},{28,24},{0,28},{5,1},{9... | collective-permute-start | bytes 393224 | tf_op jit(solution)/shard_map/ppermute | solution.py:16
  229.8 5.4 %collective-permute-start.5 = (bf16[128,512]{0,1:T(8,128)(2,1)S(1)}, bf16[128,512]{0,1:T(8,128)(2,1)S(1)}, u32[]{:S(2)}, u32[]{:S(2)}) collective-permute-start(bf16[128,512]{0,1:T(8,128)(2,1)S(1)} %get-tuple-element.9), channel_id=1, source_target_pairs={{8,0},{12,4},{16,8},{20,12},{24,16},{28,20},{0,24},{4,28},{9,1},{1... | collective-permute-start | bytes 393224 | tf_op jit(solution)/shard_map/ppermute | solution.py:16
Sparse Core Ops, SparseCore 0:
  175.6 48.3 reduce-scatter.1
where the time goes:
time: 245 us; the launch traced here: 244 us
  waiting for transfers between devices  125 us (51%)
  blocking collectives  37.9 us (15%)
  matrix products  22.3 us (9%)
  other arithmetic  19.8 us (8%)
  starting transfers between devices  16.8 us (7%)
  between operations  13.6 us (6%)
  local copies, waits for them, and re-layouts  9.21 us (4%)
    ppermute x6, waiting for transfers between devices, from_behind(): return lax.ppermute(block, axis, route)  76.3 us
    reduce_scatter x1, waiting for transfers between devices, body(): lax.psum_scatter(jnp.concatenate(pieces, axis=1), 'col', scatter_dimensio...  48.5 us
    psum x1, blocking collectives, body(): summed = lax.psum(partial_sums, 'row')  37.9 us
    ppermute x6, starting transfers between devices, from_behind(): return lax.ppermute(block, axis, route)  16.8 us
    dot_general x5, matrix products, body(): jnp.dot(strip, nearby[offset].astype(jnp.float32), precision=lax.Precisio...  12.7 us
    dot_general x6, matrix products, contract(): lax.dot_general(left_side, right_side, (((1,), (1,)), ((), ())), preferre...  9.41 us
    unnamed x30, local copies, waits for them, and re-layouts  7.84 us
  transfers between devices with their start and end apart: 7, of which 6 were waited for; matrix products, arithmetic and copies ran while one was open for 6% of the time, Pallas kernels for 0%

commit v1 on v0

--- a/solution.py
+++ b/solution.py
@@ -67,7 +67,7 @@
         )
     masked32 = masked.astype(jnp.float32)
     partial_sums = jnp.einsum("cmg,mg->cg", masked32, applied, precision=lax.Precision.HIGHEST)
-    summed = lax.psum(partial_sums, "row")
+    summed = jnp.sum(lax.all_gather(partial_sums, "row"), axis=0)
     point_density = summed[0]
     gradient = 2.0 * summed[1:]
     squared = jnp.sum(gradient * gradient, axis=0)

time: 245 us -> 242 us (0.988)
  blocking collectives: 37.9 us -> 31.1 us
  waiting for transfers between devices: 125 us -> 129 us
    psum x1 -> x0, blocking collectives: 37.9 us -> none  [body(): summed = lax.psum(partial_sums, 'row')]
    all_gather x0 -> x1, blocking collectives: none -> 31.1 us  [body(): summed = jnp.sum(lax.all_gather(partial_sums, 'row'), axis=0)]
    reduce_scatter x1, waiting for transfers between devices: 48.5 us -> 52.7 us  [body(): lax.psum_scatter(jnp.concatenate(pieces, axis=1), 'col', scatter_dimensio...]
where the time goes in v1:
time: 242 us
  waiting for transfers between devices  129 us (53%)
  blocking collectives  31.1 us (13%)
  matrix products  22.3 us (9%)
  other arithmetic  19.8 us (8%)
  starting transfers between devices  16.8 us (7%)
  between operations  13.6 us (6%)
  local copies, waits for them, and re-layouts  9.21 us (4%)
    ppermute x6, waiting for transfers between devices, from_behind(): return lax.ppermute(block, axis, route)  76.3 us
    reduce_scatter x1, waiting for transfers between devices, body(): lax.psum_scatter(jnp.concatenate(pieces, axis=1), 'col', scatter_dimensio...  52.7 us
    all_gather x1, blocking collectives, body(): summed = jnp.sum(lax.all_gather(partial_sums, 'row'), axis=0)  31.1 us
    ppermute x6, starting transfers between devices, from_behind(): return lax.ppermute(block, axis, route)  16.8 us
    dot_general x5, matrix products, body(): jnp.dot(strip, nearby[offset].astype(jnp.float32), precision=lax.Precisio...  12.7 us
    dot_general x6, matrix products, contract(): lax.dot_general(left_side, right_side, (((1,), (1,)), ((), ())), preferre...  9.4 us
    unnamed x30, local copies, waits for them, and re-layouts  7.84 us
  transfers between devices with their start and end apart: 7, of which 6 were waited for; matrix products, arithmetic and copies ran while one was open for 6% of the time, Pallas kernels for 0%

profile of v1, /device:TPU:0, one launch (start us, length us, event | category | flops | bytes accessed | tf_op | source)
XLA Modules:
  0.0 241.8 jit_solution(17568296601416926260)
XLA Ops:
  6.5 0.0 copy-start
  6.5 0.0 reduce-scatter.2.cloned.1.call-start
  6.5 0.7 convert_element_type.29
  7.2 3.3 %copy.19 = bf16[256,8,8,128]{3,2,1,0:T(8,128)(2,1)S(1)} copy(bf16[256,8,8,128]{3,1,2,0:T(8,128)(2,1)} %bitcast.66) | data formatting | bytes 8388608
  10.5 0.0 copy-start.1
  10.5 0.1 slice_multiply_fusion.1
  10.7 0.3 copy.28
  10.9 3.0 %collective-permute-start = (bf16[512,1024]{1,0:T(8,128)(2,1)S(1)}, bf16[512,1024]{1,0:T(8,128)(2,1)S(1)}, u32[]{:S(2)}, u32[]{:S(2)}) collective-permute-start(bf16[512,1024]{1,0:T(8,128)(2,1)S(1)} %bitcast.77), channel_id=1, source_target_pairs={{28,0},{0,4},{4,8},{8,12},{12,16},{16,20},{20,24},{24,28},{29,1},{... | collective-permute-start | bytes 3145736 | tf_op jit(solution)/shard_map/ppermute | solution.py:16
  14.0 3.1 %collective-permute-start.2 = (bf16[512,1024]{1,0:T(8,128)(2,1)S(1)}, bf16[512,1024]{1,0:T(8,128)(2,1)S(1)}, u32[]{:S(2)}, u32[]{:S(2)}) collective-permute-start(bf16[512,1024]{1,0:T(8,128)(2,1)S(1)} %bitcast.78), channel_id=1, source_target_pairs={{4,0},{8,4},{12,8},{16,12},{20,16},{24,20},{28,24},{0,28},{5,1},{9... | collective-permute-start | bytes 3145736 | tf_op jit(solution)/shard_map/ppermute | solution.py:16
  17.1 0.2 mul.148
  17.3 0.0 slice-start
  17.3 0.3 copy.27
  17.6 0.0 copy-done.1
  17.6 0.0 slice-start.1
  17.6 4.2 %multiply_convert_fusion = f32[4,512,1024]{2,1,0:T(8,128)} fusion(bf16[4,512,1024]{2,1,0:T(8,128)(2,1)S(1)} %copy-done.1, bf16[512,1024]{1,0:T(8,128)(2,1)S(1)} %bitcast.71), kind=kLoop, calls=%fused_computation.3 | loop fusion | flops 4194304 | bytes 13631488 | tf_op jit(solution)/shard_map/convert_element_type | solution.py:68
  21.8 37.1 %collective-permute-done = bf16[512,1024]{1,0:T(8,128)(2,1)S(1)} collective-permute-done((bf16[512,1024]{1,0:T(8,128)(2,1)S(1)}, bf16[512,1024]{1,0:T(8,128)(2,1)S(1)}, u32[]{:S(2)}, u32[]{:S(2)}) %collective-permute-start) | collective-permute-done | bytes 1048608 | tf_op jit(solution)/shard_map/ppermute | solution.py:16
  58.9 2.5 %collective-permute-start.1 = (bf16[512,1024]{1,0:T(8,128)(2,1)S(1)}, bf16[512,1024]{1,0:T(8,128)(2,1)S(1)}, u32[]{:S(2)}, u32[]{:S(2)}) collective-permute-start(bf16[512,1024]{1,0:T(8,128)(2,1)S(1)} %collective-permute-done), channel_id=1, source_target_pairs={{28,0},{0,4},{4,8},{8,12},{12,16},{16,20},{20,24},{24,28},{29,1},{... | collective-permute-start | bytes 3145736 | tf_op jit(solution)/shard_map/ppermute | solution.py:16
  61.4 0.0 slice-done
  61.4 0.0 slice-done.1
  61.4 2.2 fusion.9
  63.6 0.0 collective-permute-done.2
  63.6 0.0 copy-start.4
  63.6 3.3 %collective-permute-start.3 = (bf16[512,1024]{1,0:T(8,128)(2,1)S(1)}, bf16[512,1024]{1,0:T(8,128)(2,1)S(1)}, u32[]{:S(2)}, u32[]{:S(2)}) collective-permute-start(bf16[512,1024]{1,0:T(8,128)(2,1)S(1)} %collective-permute-done.2), channel_id=1, source_target_pairs={{4,0},{8,4},{12,8},{16,12},{20,16},{24,20},{28,24},{0,28},{5,1},{9... | collective-permute-start | bytes 3145736 | tf_op jit(solution)/shard_map/ppermute | solution.py:16
  66.9 0.0 copy-done
  66.9 0.0 copy-done.10
  66.9 0.2 convolution_bitcast_fusion
  67.1 2.2 fusion.11
  69.3 0.0 copy-done.2
  69.3 2.2 fusion.7
  71.5 0.0 copy-done.4
  71.5 33.9 %collective-permute-done.1 = bf16[512,1024]{1,0:T(8,128)(2,1)S(1)} collective-permute-done((bf16[512,1024]{1,0:T(8,128)(2,1)S(1)}, bf16[512,1024]{1,0:T(8,128)(2,1)S(1)}, u32[]{:S(2)}, u32[]{:S(2)}) %collective-permute-start.1) | collective-permute-done | bytes 1048608 | tf_op jit(solution)/shard_map/ppermute | solution.py:16
  105.4 1.1 copy-done.6
  106.5 2.2 fusion.13
  108.7 0.5 collective-permute-done.3
  109.2 3.9 %add_add_fusion = f32[1024,512]{1,0:T(8,128)} fusion(f32[1024,512]{1,0:T(8,128)S(1)} %fusion.7, f32[1024,512]{1,0:T(8,128)S(1)} %fusion.9, f32[1024,512]{1,0:T(8,128)S(1)} %fusion.13, f32[1024,512]{1,0:T(8,128)S(1)} %fusion.11, bf16[512,1024]{1,0:T(8,128)(2,1)S(1)} %collective-permute-done.3, f32[512,2560]{1,0:T(8,128)S(1)} %bitcast.75), kind=kOutput, calls=%fused_computation.9 | convolution fusion | flops 3223322624 | bytes 12582912 | tf_op jit(solution)/shard_map/dot_general | solution.py:65
  113.1 2.9 %copy.17 = f32[1024,512]{0,1:T(8,128)} copy(f32[1024,512]{1,0:T(8,128)} %add_add_fusion) | data formatting | bytes 4194304
  116.0 4.3 %multiply_reduce_fusion = f32[1024,4]{0,1:T(4,128)S(1)} fusion(f32[1024,512]{0,1:T(8,128)} %copy.17, bf16[4,512,1024]{2,1,0:T(8,128)(2,1)} %param.7, bf16[512,1024]{1,0:T(8,128)(2,1)S(1)} %bitcast.72), kind=kLoop, calls=%fused_computation | loop fusion | flops 8384512 | bytes 7356416 | tf_op jit(solution)/shard_map/cmg,mg->cg/dot_general | solution.py:69
  120.3 31.1 %all-gather.1 = f32[8,4,1024]{2,1,0:T(4,128)S(1)} all-gather(f32[1,4,1024]{2,1,0:T(4,128)S(1)} %bitcast.79), channel_id=2, replica_groups=mesh['row'=8,'col'=4] {'row'}, dimensions={0}, use_global_device_ids=true | all-gather | bytes 147456 | tf_op jit(solution)/shard_map/all_gather | solution.py:70
  151.5 0.0 copy-done.8
  151.5 0.0 copy-done.9
  151.5 0.1 multiply_multiply_fusion
  151.6 3.9 %fusion = f32[512,1024]{1,0:T(8,128)S(1)} fusion(f32[4,512,1024]{2,1,0:T(8,128)} %multiply_convert_fusion, f32[3,1024]{1,0:T(4,128)S(1)} %slice_multiply_fusion.2), kind=kLoop, calls=%fused_computation.2 | loop fusion | flops 2621440 | bytes 8400896 | tf_op jit(solution)/shard_map/reduce_sum | solution.py:87
  155.5 1.9 fusion.2
  157.4 1.9 fusion.5
  159.3 0.0 copy-start.5
  159.3 0.8 fusion.17
  160.1 1.7 fusion.4
  161.8 0.0 copy-done.5
  161.8 1.7 convolution_dynamic-update-slice_fusion.3
  163.6 1.7 convolution_dynamic-update-slice_fusion.2
  165.3 0.0 copy-done.3
  165.3 1.7 convolution_dynamic-update-slice_fusion.1
  167.0 0.0 copy-done.7
  167.0 1.7 convolution_dynamic-update-slice_fusion
  168.8 0.0 reduce-scatter.2.cloned.1.call-update
  168.8 52.7 %reduce-scatter.2.cloned.1.call-done = f32[128,2560]{0,1:T(8,128)} async-done(((f32[512,2560]{0,1:T(8,128)}), f32[128,2560]{0,1:T(8,128)}) %reduce-scatter.2.cloned.1.call-update) | async-done | bytes 1310736 | tf_op jit(solution)/shard_map/reduce_scatter | solution.py:95
  221.4 1.4 convert.4
  222.9 4.3 %collective-permute-start.4 = (bf16[128,512]{0,1:T(8,128)(2,1)S(1)}, bf16[128,512]{0,1:T(8,128)(2,1)S(1)}, u32[]{:S(2)}, u32[]{:S(2)}) collective-permute-start(bf16[128,512]{0,1:T(8,128)(2,1)S(1)} %get-tuple-element.8), channel_id=1, source_target_pairs={{4,0},{8,4},{12,8},{16,12},{20,16},{24,20},{28,24},{0,28},{5,1},{9... | collective-permute-start | bytes 393224 | tf_op jit(solution)/shard_map/ppermute | solution.py:16
  227.2 0.5 collective-permute-start.5
  227.7 3.4 %collective-permute-done.4 = bf16[128,512]{0,1:T(8,128)(2,1)S(1)} collective-permute-done((bf16[128,512]{0,1:T(8,128)(2,1)S(1)}, bf16[128,512]{0,1:T(8,128)(2,1)S(1)}, u32[]{:S(2)}, u32[]{:S(2)}) %collective-permute-start.4) | collective-permute-done | bytes 131104 | tf_op jit(solution)/shard_map/ppermute | solution.py:16
  231.0 1.5 collective-permute-done.5
  232.6 1.2 fusion.18
  233.7 0.1 pad_maximum_fusion
  233.8 1.1 copy.9
  (13 shorter events, 0.1 us)
Async XLA Ops:
  6.5 60.4 %copy-start = (f32[64]{0:T(128)S(1)}, f32[64]{0:T(128)}, u32[]{:S(2)}) copy-start(f32[64]{0:T(128)} %param.11) | copy-start | bytes 772
  6.5 214.9 %reduce-scatter.2.cloned.1.call-start = ((), (), s32[]{:S(2)}) async-start(), calls=%async_computation.1 | async-start | bytes 6553600 | tf_op jit(solution)/shard_map/reduce_scatter | solution.py:95
  10.5 7.1 %copy-start.1 = (bf16[4,512,1024]{2,1,0:T(8,128)(2,1)S(1)}, bf16[4,512,1024]{2,1,0:T(8,128)(2,1)}, u32[]{:S(2)}) copy-start(bf16[4,512,1024]{2,1,0:T(8,128)(2,1)} %param.7) | copy-start | bytes 12582916
  10.9 47.9 %collective-permute-start = (bf16[512,1024]{1,0:T(8,128)(2,1)S(1)}, bf16[512,1024]{1,0:T(8,128)(2,1)S(1)}, u32[]{:S(2)}, u32[]{:S(2)}) collective-permute-start(bf16[512,1024]{1,0:T(8,128)(2,1)S(1)} %bitcast.77), channel_id=1, source_target_pairs={{28,0},{0,4},{4,8},{8,12},{12,16},{16,20},{20,24},{24,28},{29,1},{... | collective-permute-start | bytes 3145736 | tf_op jit(solution)/shard_map/ppermute | solution.py:16
  14.0 49.6 %collective-permute-start.2 = (bf16[512,1024]{1,0:T(8,128)(2,1)S(1)}, bf16[512,1024]{1,0:T(8,128)(2,1)S(1)}, u32[]{:S(2)}, u32[]{:S(2)}) collective-permute-start(bf16[512,1024]{1,0:T(8,128)(2,1)S(1)} %bitcast.78), channel_id=1, source_target_pairs={{4,0},{8,4},{12,8},{16,12},{20,16},{24,20},{28,24},{0,28},{5,1},{9... | collective-permute-start | bytes 3145736 | tf_op jit(solution)/shard_map/ppermute | solution.py:16
  17.3 44.1 %slice-start = ((s8[5242880]{0:T(1024)(128)(4,1)}), s8[4194304]{0:T(1024)(128)(4,1)S(1)}, s32[]{:S(2)}) async-start(s8[5242880]{0:T(1024)(128)(4,1)} %bitcast.74), calls=%async_computation.2 | async-start | bytes 8388608
  17.6 43.8 %slice-start.1 = ((s8[5242880]{0:T(1024)(128)(4,1)}), s8[1048576]{0:T(1024)(128)(4,1)S(1)}, s32[]{:S(2)}) async-start(s8[5242880]{0:T(1024)(128)(4,1)} %bitcast.74), calls=%async_computation.3 | async-start | bytes 2097152
  21.8 45.1 %copy-start.10 = (s32[8]{0:T(128)S(1)}, s32[8]{0:T(128)}, u32[]{:S(2)}) copy-start(s32[8]{0:T(128)} %param.10) | copy-start | bytes 100
  58.9 10.4 %copy-start.2 = (bf16[512,1024]{1,0:T(8,128)(2,1)}, bf16[512,1024]{1,0:T(8,128)(2,1)S(1)}, u32[]{:S(2)}) copy-start(bf16[512,1024]{1,0:T(8,128)(2,1)S(1)} %collective-permute-done) | copy-start | bytes 3145732
  58.9 46.5 %collective-permute-start.1 = (bf16[512,1024]{1,0:T(8,128)(2,1)S(1)}, bf16[512,1024]{1,0:T(8,128)(2,1)S(1)}, u32[]{:S(2)}, u32[]{:S(2)}) collective-permute-start(bf16[512,1024]{1,0:T(8,128)(2,1)S(1)} %collective-permute-done), channel_id=1, source_target_pairs={{28,0},{0,4},{4,8},{8,12},{12,16},{16,20},{20,24},{24,28},{29,1},{... | collective-permute-start | bytes 3145736 | tf_op jit(solution)/shard_map/ppermute | solution.py:16
  63.6 7.9 %copy-start.4 = (bf16[512,1024]{1,0:T(8,128)(2,1)}, bf16[512,1024]{1,0:T(8,128)(2,1)S(1)}, u32[]{:S(2)}) copy-start(bf16[512,1024]{1,0:T(8,128)(2,1)S(1)} %collective-permute-done.2) | copy-start | bytes 3145732
  63.6 45.6 %collective-permute-start.3 = (bf16[512,1024]{1,0:T(8,128)(2,1)S(1)}, bf16[512,1024]{1,0:T(8,128)(2,1)S(1)}, u32[]{:S(2)}, u32[]{:S(2)}) collective-permute-start(bf16[512,1024]{1,0:T(8,128)(2,1)S(1)} %collective-permute-done.2), channel_id=1, source_target_pairs={{4,0},{8,4},{12,8},{16,12},{20,16},{24,20},{28,24},{0,28},{5,1},{9... | collective-permute-start | bytes 3145736 | tf_op jit(solution)/shard_map/ppermute | solution.py:16
  105.4 1.1 copy-start.6
  116.0 35.5 %copy-start.8 = (f32[1024]{0:T(1024)S(1)}, f32[1024]{0:T(1024)}, u32[]{:S(2)}) copy-start(f32[1024]{0:T(1024)} %param.12) | copy-start | bytes 12292
  116.0 35.5 %copy-start.9 = (f32[1024]{0:T(1024)S(1)}, f32[1024]{0:T(1024)}, u32[]{:S(2)}) copy-start(f32[1024]{0:T(1024)} %param.13) | copy-start | bytes 12292
  159.3 2.5 %copy-start.5 = (bf16[512,1024]{1,0:T(8,128)(2,1)S(1)}, bf16[512,1024]{1,0:T(8,128)(2,1)}, u32[]{:S(2)}) copy-start(bf16[512,1024]{1,0:T(8,128)(2,1)} %copy-done.4) | copy-start | bytes 3145732
  161.8 3.5 %copy-start.3 = (bf16[512,1024]{1,0:T(8,128)(2,1)S(1)}, bf16[512,1024]{1,0:T(8,128)(2,1)}, u32[]{:S(2)}) copy-start(bf16[512,1024]{1,0:T(8,128)(2,1)} %copy-done.2) | copy-start | bytes 3145732
  163.6 3.5 %copy-start.7 = (bf16[512,1024]{1,0:T(8,128)(2,1)S(1)}, bf16[512,1024]{1,0:T(8,128)(2,1)}, u32[]{:S(2)}) copy-start(bf16[512,1024]{1,0:T(8,128)(2,1)} %copy-done.6) | copy-start | bytes 3145732
  222.9 8.2 %collective-permute-start.4 = (bf16[128,512]{0,1:T(8,128)(2,1)S(1)}, bf16[128,512]{0,1:T(8,128)(2,1)S(1)}, u32[]{:S(2)}, u32[]{:S(2)}) collective-permute-start(bf16[128,512]{0,1:T(8,128)(2,1)S(1)} %get-tuple-element.8), channel_id=1, source_target_pairs={{4,0},{8,4},{12,8},{16,12},{20,16},{24,20},{28,24},{0,28},{5,1},{9... | collective-permute-start | bytes 393224 | tf_op jit(solution)/shard_map/ppermute | solution.py:16
  227.2 5.4 %collective-permute-start.5 = (bf16[128,512]{0,1:T(8,128)(2,1)S(1)}, bf16[128,512]{0,1:T(8,128)(2,1)S(1)}, u32[]{:S(2)}, u32[]{:S(2)}) collective-permute-start(bf16[128,512]{0,1:T(8,128)(2,1)S(1)} %get-tuple-element.9), channel_id=1, source_target_pairs={{8,0},{12,4},{16,8},{20,12},{24,16},{28,20},{0,24},{4,28},{9,1},{1... | collective-permute-start | bytes 393224 | tf_op jit(solution)/shard_map/ppermute | solution.py:16
Sparse Core Ops, SparseCore 0:
  168.9 52.4 reduce-scatter.1
